TPU v7x, 512 devices: a whole 4x8x8 slice. The times are simulated.
512 devices in a mesh: chain: 64 (over y, x, core), cols: 8 (over z).
Axes of the slice: x: 4, y: 8, z: 8, core: 2. Of those that a mesh axis runs over, the one named last changes fastest.
Arguments:
- start_vectors: float32 [1024, 256, 256], P('chain', 'cols'), may hold values from -6 to 6
- factors: float32 [1024, 256, 256], P('chain', 'cols'), may hold values from -1.2 to 1.2, as said below
Outputs:
- vectors: float32 [1024, 256, 256], P('chain', 'cols')
- log_growth: float32 [256], P('cols')
Inputs may be any that keep to these rules, and one draw needn't show every extreme that they name: `factors`: the factor blocks of the shifted operator; every product of consecutive factor blocks is bounded.
All inputs are finite; a program needn't handle non-finite values.
Results may differ from a plain program's by a relative error of at most 0.0003.
Values sent between devices are 32-bit elements; how exact they have to be, the bound alone decides.
No kernel may reach another device: no remote copies, remote signals or barrier semaphores. Data moves between devices by JAX's collectives and lax.ppermute only.
A program may use at most 128 MiB of HBM per device.

v0:
```python
import jax
import jax.numpy as jnp
from jax import lax
from jax.sharding import PartitionSpec as P

eps_value = 1e-06


def from_behind(block, axis, distance):
    devices = range(lax.axis_size(axis))
    route = [(i - distance, i) for i in devices if i - distance in devices]
    return lax.ppermute(block, axis, route)


def transform(matrix, vectors_in):
    return lax.dot_general(
        vectors_in,
        matrix,
        (((1,), (1,)), ((), ())),
        precision=lax.Precision.HIGHEST,
        preferred_element_type=jnp.float32,
    )


def compose(later, earlier):
    return jnp.dot(
        later, earlier, precision=lax.Precision.HIGHEST, preferred_element_type=jnp.float32
    )


def forward_rows(factors, right_side, incoming):

    def forward_advance(carried, element):
        matrix, source = element
        carried = transform(matrix, carried) + source
        return (carried, carried)

    return lax.scan(forward_advance, incoming, (factors, right_side))


def backward_rows(factors, forward, incoming):

    def backward_advance(carried, element):
        matrix, source = element
        carried = transform(matrix, source + carried)
        return (carried, carried)

    return lax.scan(backward_advance, incoming, (factors, forward), reverse=True)


def chain_operator(factors, reverse):
    identity_block = jnp.eye(factors.shape[1], dtype=jnp.float32)

    def chain_advance(running, matrix):
        return (compose(matrix, running), None)

    running, _ = lax.scan(chain_advance, identity_block, factors, reverse=reverse)
    return running


def section_count():
    return (lax.axis_size("chain") - 1).bit_length()


def enter_state(summary, direction):
    return from_behind(summary, "chain", direction)


def solve_system(factors, right_side, prefix_forward, prefix_backward):
    zero_state = jnp.zeros(right_side.shape[1:], jnp.float32)
    local_last, _ = forward_rows(factors, right_side, zero_state)
    incoming = enter_state(prefix_forward(local_last), 1)
    _, forward = forward_rows(factors, right_side, incoming)
    local_first, _ = backward_rows(factors, forward, zero_state)
    incoming_back = enter_state(prefix_backward(local_first), -1)
    _, solved = backward_rows(factors, forward, incoming_back)
    return solved


def shards(start_vectors, factors):
    full_factors = lax.all_gather(factors, "cols", axis=1, tiled=True)

    def pair_prefix(operator, summary, direction):
        sections = section_count()
        for section_index in range(sections):
            distance = direction * (1 << section_index)
            if section_index + 1 < sections:
                received_op, received_sum = from_behind((operator, summary), "chain", distance)
                summary = transform(operator, received_sum) + summary
                operator = compose(operator, received_op)
            else:
                received_sum = from_behind(summary, "chain", distance)
                summary = transform(operator, received_sum) + summary
        return summary

    def prefix_forward(summary):
        return pair_prefix(chain_operator(full_factors, False), summary, 1)

    def prefix_backward(summary):
        return pair_prefix(chain_operator(full_factors, True), summary, -1)

    cell_count = start_vectors.shape[0] * lax.axis_size("chain") * start_vectors.shape[2]
    first_solve = solve_system(full_factors, start_vectors, prefix_forward, prefix_backward)
    first_squares = lax.psum(jnp.sum(first_solve * first_solve, axis=(0, 2)), "chain")
    scale_one = jnp.sqrt(first_squares / cell_count + eps_value)
    second_solve = solve_system(
        full_factors, first_solve / scale_one[None, :, None], prefix_forward, prefix_backward
    )
    second_squares = lax.psum(jnp.sum(second_solve * second_solve, axis=(0, 2)), "chain")
    scale_two = jnp.sqrt(second_squares / cell_count + eps_value)
    result_vectors = second_solve / scale_two[None, :, None]
    return (result_vectors, jnp.log(scale_two))


def solution(mesh):
    return jax.shard_map(
        shards,
        mesh=mesh,
        in_specs=(P("chain", "cols", None), P("chain", "cols", None)),
        out_specs=(P("chain", "cols", None), P("cols")),
        check_vma=False,
    )
```

profile of v0, /device:TPU:32, one launch (start us, length us, event | category | flops | bytes accessed | tf_op | source)
XLA Modules:
  0.0 812.4 jit_solution(6026892274242298097)
XLA Ops:
  8.0 64.7 %all-gather.2.cloned.1.call-done = f32[16,256,256]{2,1,0:T(8,128)} async-done(((f32[16,32,256]{2,1,0:T(8,128)}), f32[16,256,256]{2,1,0:T(8,128)}) %all-gather.2.cloned.1.call-update) | async-done | bytes 4194320 | tf_op jit(solution)/shard_map/all_gather | solution.py:81
  72.7 21.4 %while.146 = (s32[]{:T(128)}, f32[32,256]{1,0:T(8,128)S(1)}, f32[16,256,256]{2,1,0:T(8,128)}, f32[16,32,256]{2,1,0:T(8,128)}, s32[]{:T(128)}, /*index=5*/s32[]{:T(128)}) while((s32[]{:T(128)}, f32[32,256]{1,0:T(8,128)S(1)}, f32[16,256,256]{2,1,0:T(8,128)}, f32[16,32,256]{2,1,0:T(8,128)}, s32[]{:T(128)}, /*index=5*/s32[]{:T(128)}) %tuple.241), condition=%wide.region_1.2_spmd.clone, body=%wide.region_0.1_spmd.clone.sunk | while | flops 25182212 | bytes 427087 | solution.py:38
  96.0 22.1 %while.138 = (s32[]{:T(128)}, f32[256,256]{1,0:T(8,128)S(1)}, f32[16,256,256]{2,1,0:T(8,128)}, s32[]{:T(128)}) while((s32[]{:T(128)}, f32[256,256]{1,0:T(8,128)S(1)}, f32[16,256,256]{2,1,0:T(8,128)}, s32[]{:T(128)}) %tuple.273), condition=%wide.region_3.4_spmd, body=%wide.region_2.3_spmd.sunk | while | flops 201326592 | bytes 1311285 | solution.py:57
  134.6 7.3 collective-permute-done.4
  146.4 10.8 %collective-permute-done.6 = f32[256,256]{1,0:T(8,128)S(1)} collective-permute-done((f32[256,256]{1,0:T(8,128)S(1)}, f32[256,256]{1,0:T(8,128)S(1)}, u32[]{:S(2)}, u32[]{:S(2)}) %collective-permute-start.6) | collective-permute-done | bytes 262176 | tf_op jit(solution)/shard_map/ppermute | solution.py:12
  161.9 7.5 collective-permute-done.8
  173.3 7.5 collective-permute-done.10
  190.7 21.4 %while.139 = (s32[]{:T(128)}, f32[32,256]{1,0:T(8,128)S(1)}, f32[16,32,256]{2,1,0:T(8,128)S(1)}, f32[16,256,256]{2,1,0:T(8,128)}, f32[16,32,256]{2,1,0:T(8,128)}, /*index=5*/s32[]{:T(128)}) while((s32[]{:T(128)}, f32[32,256]{1,0:T(8,128)S(1)}, f32[16,32,256]{2,1,0:T(8,128)S(1)}, f32[16,256,256]{2,1,0:T(8,128)}, f32[16,32,256]{2,1,0:T(8,128)}, ...), condition=%wide.region_5.6_spmd, body=%wide.region_4.5_spmd.sunk | while | flops 25174016 | bytes 459845 | solution.py:38
  212.1 21.3 %while.140 = (s32[]{:T(128)}, f32[32,256]{1,0:T(8,128)S(1)}, f32[16,32,256]{2,1,0:T(8,128)S(1)}, f32[16,256,256]{2,1,0:T(8,128)}, s32[]{:T(128)}, /*index=5*/s32[]{:T(128)}) while((s32[]{:T(128)}, f32[32,256]{1,0:T(8,128)S(1)}, f32[16,32,256]{2,1,0:T(8,128)S(1)}, f32[16,256,256]{2,1,0:T(8,128)}, s32[]{:T(128)}, /*index=5*/s32[]{:T(128)}) %tuple.275), condition=%wide.region_7.8_spmd, body=%wide.region_6.7_spmd.sunk | while | flops 25174020 | bytes 427089 | solution.py:48
  235.4 22.1 %while.141 = (s32[]{:T(128)}, f32[256,256]{1,0:T(8,128)S(1)}, f32[16,256,256]{2,1,0:T(8,128)}, s32[]{:T(128)}, s32[]{:T(128)}) while((s32[]{:T(128)}, f32[256,256]{1,0:T(8,128)S(1)}, f32[16,256,256]{2,1,0:T(8,128)}, s32[]{:T(128)}, s32[]{:T(128)}) %tuple.276), condition=%wide.region_9.10_spmd, body=%wide.region_8.9_spmd.sunk | while | flops 201326592 | bytes 1310797 | solution.py:57
  278.5 7.5 collective-permute-done.18
  290.7 6.7 collective-permute-done.20
  301.4 13.4 %collective-permute-done.22 = f32[256,256]{1,0:T(8,128)S(1)} collective-permute-done((f32[256,256]{1,0:T(8,128)S(1)}, f32[256,256]{1,0:T(8,128)S(1)}, u32[]{:S(2)}, u32[]{:S(2)}) %collective-permute-start.22) | collective-permute-done | bytes 262176 | tf_op jit(solution)/shard_map/ppermute | solution.py:12
  322.7 21.6 %while.142 = (s32[]{:T(128)}, f32[32,256]{1,0:T(8,128)S(1)}, f32[16,32,256]{2,1,0:T(8,128)S(1)}, f32[16,32,256]{2,1,0:T(8,128)}, f32[16,256,256]{2,1,0:T(8,128)}, /*index=5*/s32[]{:T(128)}, s32[]{:T(128)}) while((s32[]{:T(128)}, f32[32,256]{1,0:T(8,128)S(1)}, f32[16,32,256]{2,1,0:T(8,128)S(1)}, f32[16,32,256]{2,1,0:T(8,128)}, ...), condition=%wide.region_11.12_spmd, body=%wide.region_10.11_spmd.sunk | while | flops 25174020 | bytes 460377 | solution.py:48
  344.5 129.1 %psum.14 = f32[32]{0:T(128)S(1)} all-reduce(f32[32]{0:T(128)S(1)} %multiply_reduce_fusion.1), channel_id=1, replica_groups=mesh['chain'=64,'cols'=8] {'chain'}, use_global_device_ids=true, to_apply=%region_13.14 | all-reduce | flops 32 | bytes 256 | tf_op jit(solution)/shard_map/psum | solution.py:104
  474.5 21.5 %while.147 = (s32[]{:T(128)}, f32[32,256]{1,0:T(8,128)S(1)}, f32[16,256,256]{2,1,0:T(8,128)}, f32[16,32,256]{2,1,0:T(8,128)}, s32[]{:T(128)}, /*index=5*/s32[]{:T(128)}) while((s32[]{:T(128)}, f32[32,256]{1,0:T(8,128)S(1)}, f32[16,256,256]{2,1,0:T(8,128)}, f32[16,32,256]{2,1,0:T(8,128)}, s32[]{:T(128)}, ...), condition=%wide.region_15.16_spmd.clone, body=%wide.region_14.15_spmd.clone.sunk | while | flops 25182212 | bytes 427087 | solution.py:38
  506.8 7.2 collective-permute-done.25
  516.4 7.5 collective-permute-done.26
  541.4 8.2 %collective-permute-done.29 = f32[32,256]{1,0:T(8,128)S(1)} collective-permute-done((f32[32,256]{1,0:T(8,128)S(1)}, f32[32,256]{1,0:T(8,128)S(1)}, u32[]{:S(2)}, u32[]{:S(2)}) %collective-permute-start.29) | collective-permute-done | bytes 32800 | tf_op jit(solution)/shard_map/ppermute | solution.py:12
  558.6 21.4 %while.143 = (s32[]{:T(128)}, f32[32,256]{1,0:T(8,128)S(1)}, f32[16,32,256]{2,1,0:T(8,128)S(1)}, f32[16,256,256]{2,1,0:T(8,128)}, f32[16,32,256]{2,1,0:T(8,128)}, /*index=5*/s32[]{:T(128)}) while((s32[]{:T(128)}, f32[32,256]{1,0:T(8,128)S(1)}, f32[16,32,256]{2,1,0:T(8,128)S(1)}, f32[16,256,256]{2,1,0:T(8,128)}, f32[16,32,256]{2,1,0:T(8,128)}, ...), condition=%wide.region_17.18_spmd, body=%wide.region_16.17_spmd.sunk | while | flops 25174016 | bytes 459845 | solution.py:38
  580.0 21.3 %while.144 = (s32[]{:T(128)}, f32[32,256]{1,0:T(8,128)S(1)}, f32[16,32,256]{2,1,0:T(8,128)S(1)}, f32[16,256,256]{2,1,0:T(8,128)}, s32[]{:T(128)}, /*index=5*/s32[]{:T(128)}) while((s32[]{:T(128)}, f32[32,256]{1,0:T(8,128)S(1)}, f32[16,32,256]{2,1,0:T(8,128)S(1)}, f32[16,256,256]{2,1,0:T(8,128)}, s32[]{:T(128)}, /*index=5*/s32[]{:T(128)}) %tuple.280), condition=%wide.region_19.20_spmd, body=%wide.region_18.19_spmd.sunk | while | flops 25174020 | bytes 427089 | solution.py:48
  635.6 16.2 %collective-permute-start.37 = (f32[32,256]{1,0:T(8,128)S(1)}, f32[32,256]{1,0:T(8,128)S(1)}, u32[]{:S(2)}, u32[]{:S(2)}) collective-permute-start(f32[32,256]{1,0:T(8,128)S(1)} %convolution_add_fusion), channel_id=1, source_target_pairs={{8,0},{16,8},{24,16},{32,24},{40,32},{48,40},{56,48},{64,56},{72,6... | collective-permute-start | bytes 98312 | tf_op jit(solution)/shard_map/ppermute | solution.py:12
  653.5 21.3 %while.145 = (s32[]{:T(128)}, f32[32,256]{1,0:T(8,128)S(1)}, f32[16,32,256]{2,1,0:T(8,128)S(1)}, f32[16,32,256]{2,1,0:T(8,128)S(1)}, f32[16,256,256]{2,1,0:T(8,128)}, /*index=5*/s32[]{:T(128)}, s32[]{:T(128)}) while((s32[]{:T(128)}, f32[32,256]{1,0:T(8,128)S(1)}, f32[16,32,256]{2,1,0:T(8,128)S(1)}, f32[16,32,256]{2,1,0:T(8,128)S(1)}, ...), condition=%wide.region_21.22_spmd, body=%wide.region_20.21_spmd.sunk | while | flops 25174020 | bytes 460377 | solution.py:48
  675.0 129.1 %psum.15 = f32[32]{0:T(128)S(1)} all-reduce(f32[32]{0:T(128)S(1)} %multiply_reduce_fusion), channel_id=1, replica_groups=mesh['chain'=64,'cols'=8] {'chain'}, use_global_device_ids=true, to_apply=%region_23.24 | all-reduce | flops 32 | bytes 256 | tf_op jit(solution)/shard_map/psum | solution.py:109
  (443 shorter events, 369.9 us)
Async XLA Ops:
  7.2 65.5 %all-gather.2.cloned.1.call-start = ((), (), s32[]{:S(2)}) async-start(), calls=%async_computation | async-start | bytes 4718592 | tf_op jit(solution)/shard_map/all_gather | solution.py:81
  94.1 27.5 %collective-permute-start = (f32[32,256]{1,0:T(8,128)S(1)}, f32[32,256]{1,0:T(8,128)S(1)}, u32[]{:S(2)}, u32[]{:S(2)}) collective-permute-start(f32[32,256]{1,0:T(8,128)S(1)} %get-tuple-element.568), channel_id=1, source_target_pairs={{0,8},{8,16},{16,24},{24,32},{32,40},{40,48},{48,56},{56,64},{64,7... | collective-permute-start | bytes 98312 | tf_op jit(solution)/shard_map/ppermute | solution.py:12
  118.1 11.0 %collective-permute-start.2 = (f32[256,256]{1,0:T(8,128)S(1)}, f32[256,256]{1,0:T(8,128)S(1)}, u32[]{:S(2)}, u32[]{:S(2)}) collective-permute-start(f32[256,256]{1,0:T(8,128)S(1)} %get-tuple-element.569), channel_id=1, source_target_pairs={{0,8},{8,16},{16,24},{24,32},{32,40},{40,48},{48,56},{56,64},{64,7... | collective-permute-start | bytes 786440 | tf_op jit(solution)/shard_map/ppermute | solution.py:12
  122.0 9.5 %collective-permute-start.1 = (f32[32,256]{1,0:T(8,128)S(1)}, f32[32,256]{1,0:T(8,128)S(1)}, u32[]{:S(2)}, u32[]{:S(2)}) collective-permute-start(f32[32,256]{1,0:T(8,128)S(1)} %convolution_add_fusion.23), channel_id=1, source_target_pairs={{0,16},{8,24},{16,32},{24,40},{32,48},{40,56},{48,64},{56,72},{64,... | collective-permute-start | bytes 98312 | tf_op jit(solution)/shard_map/ppermute | solution.py:12
  129.5 12.3 %collective-permute-start.4 = (f32[256,256]{1,0:T(8,128)S(1)}, f32[256,256]{1,0:T(8,128)S(1)}, u32[]{:S(2)}, u32[]{:S(2)}) collective-permute-start(f32[256,256]{1,0:T(8,128)S(1)} %fusion.54), channel_id=1, source_target_pairs={{0,16},{8,24},{16,32},{24,40},{32,48},{40,56},{48,64},{56,72},{64,... | collective-permute-start | bytes 786440 | tf_op jit(solution)/shard_map/ppermute | solution.py:12
  131.8 12.3 %collective-permute-start.3 = (f32[32,256]{1,0:T(8,128)S(1)}, f32[32,256]{1,0:T(8,128)S(1)}, u32[]{:S(2)}, u32[]{:S(2)}) collective-permute-start(f32[32,256]{1,0:T(8,128)S(1)} %convolution_add_fusion.22), channel_id=1, source_target_pairs={{0,32},{8,40},{16,48},{24,56},{32,64},{40,72},{48,80},{56,88},{64,... | collective-permute-start | bytes 98312 | tf_op jit(solution)/shard_map/ppermute | solution.py:12
  142.2 15.0 %collective-permute-start.6 = (f32[256,256]{1,0:T(8,128)S(1)}, f32[256,256]{1,0:T(8,128)S(1)}, u32[]{:S(2)}, u32[]{:S(2)}) collective-permute-start(f32[256,256]{1,0:T(8,128)S(1)} %fusion.55), channel_id=1, source_target_pairs={{0,32},{8,40},{16,48},{24,56},{32,64},{40,72},{48,80},{56,88},{64,... | collective-permute-start | bytes 786440 | tf_op jit(solution)/shard_map/ppermute | solution.py:12
  144.5 15.1 %collective-permute-start.5 = (f32[32,256]{1,0:T(8,128)S(1)}, f32[32,256]{1,0:T(8,128)S(1)}, u32[]{:S(2)}, u32[]{:S(2)}) collective-permute-start(f32[32,256]{1,0:T(8,128)S(1)} %convolution_add_fusion.21), channel_id=1, source_target_pairs={{0,64},{8,72},{16,80},{24,88},{32,96},{40,104},{48,112},{56,120},{... | collective-permute-start | bytes 98312 | tf_op jit(solution)/shard_map/ppermute | solution.py:12
  157.6 11.7 %collective-permute-start.8 = (f32[256,256]{1,0:T(8,128)S(1)}, f32[256,256]{1,0:T(8,128)S(1)}, u32[]{:S(2)}, u32[]{:S(2)}) collective-permute-start(f32[256,256]{1,0:T(8,128)S(1)} %fusion.56), channel_id=1, source_target_pairs={{0,64},{8,72},{16,80},{24,88},{32,96},{40,104},{48,112},{56,120},{... | collective-permute-start | bytes 786440 | tf_op jit(solution)/shard_map/ppermute | solution.py:12
  159.9 11.7 %collective-permute-start.7 = (f32[32,256]{1,0:T(8,128)S(1)}, f32[32,256]{1,0:T(8,128)S(1)}, u32[]{:S(2)}, u32[]{:S(2)}) collective-permute-start(f32[32,256]{1,0:T(8,128)S(1)} %convolution_add_fusion.20), channel_id=1, source_target_pairs={{0,128},{8,136},{16,144},{24,152},{32,160},{40,168},{48,176},{56,1... | collective-permute-start | bytes 98312 | tf_op jit(solution)/shard_map/ppermute | solution.py:12
  169.7 11.1 %collective-permute-start.10 = (f32[256,256]{1,0:T(8,128)S(1)}, f32[256,256]{1,0:T(8,128)S(1)}, u32[]{:S(2)}, u32[]{:S(2)}) collective-permute-start(f32[256,256]{1,0:T(8,128)S(1)} %fusion.57), channel_id=1, source_target_pairs={{0,128},{8,136},{16,144},{24,152},{32,160},{40,168},{48,176},{56,1... | collective-permute-start | bytes 786440 | tf_op jit(solution)/shard_map/ppermute | solution.py:12
  172.0 9.7 %collective-permute-start.9 = (f32[32,256]{1,0:T(8,128)S(1)}, f32[32,256]{1,0:T(8,128)S(1)}, u32[]{:S(2)}, u32[]{:S(2)}) collective-permute-start(f32[32,256]{1,0:T(8,128)S(1)} %convolution_add_fusion.19), channel_id=1, source_target_pairs={{0,256},{8,264},{16,272},{24,280},{32,288},{40,296},{48,304},{56,3... | collective-permute-start | bytes 98312 | tf_op jit(solution)/shard_map/ppermute | solution.py:12
  233.5 26.0 %collective-permute-start.12 = (f32[32,256]{1,0:T(8,128)S(1)}, f32[32,256]{1,0:T(8,128)S(1)}, u32[]{:S(2)}, u32[]{:S(2)}) collective-permute-start(f32[32,256]{1,0:T(8,128)S(1)} %get-tuple-element.571), channel_id=1, source_target_pairs={{8,0},{16,8},{24,16},{32,24},{40,32},{48,40},{56,48},{64,56},{72,6... | collective-permute-start | bytes 98312 | tf_op jit(solution)/shard_map/ppermute | solution.py:12
  264.1 9.8 %collective-permute-start.16 = (f32[256,256]{1,0:T(8,128)S(1)}, f32[256,256]{1,0:T(8,128)S(1)}, u32[]{:S(2)}, u32[]{:S(2)}) collective-permute-start(f32[256,256]{1,0:T(8,128)S(1)} %fusion.59), channel_id=1, source_target_pairs={{16,0},{24,8},{32,16},{40,24},{48,32},{56,40},{64,48},{72,56},{80,... | collective-permute-start | bytes 786440 | tf_op jit(solution)/shard_map/ppermute | solution.py:12
  266.9 9.2 %collective-permute-start.15 = (f32[32,256]{1,0:T(8,128)S(1)}, f32[32,256]{1,0:T(8,128)S(1)}, u32[]{:S(2)}, u32[]{:S(2)}) collective-permute-start(f32[32,256]{1,0:T(8,128)S(1)} %convolution_add_fusion.16), channel_id=1, source_target_pairs={{32,0},{40,8},{48,16},{56,24},{64,32},{72,40},{80,48},{88,56},{96,... | collective-permute-start | bytes 98312 | tf_op jit(solution)/shard_map/ppermute | solution.py:12
  274.3 11.7 %collective-permute-start.18 = (f32[256,256]{1,0:T(8,128)S(1)}, f32[256,256]{1,0:T(8,128)S(1)}, u32[]{:S(2)}, u32[]{:S(2)}) collective-permute-start(f32[256,256]{1,0:T(8,128)S(1)} %fusion.60), channel_id=1, source_target_pairs={{32,0},{40,8},{48,16},{56,24},{64,32},{72,40},{80,48},{88,56},{96,... | collective-permute-start | bytes 786440 | tf_op jit(solution)/shard_map/ppermute | solution.py:12
  276.5 11.9 %collective-permute-start.17 = (f32[32,256]{1,0:T(8,128)S(1)}, f32[32,256]{1,0:T(8,128)S(1)}, u32[]{:S(2)}, u32[]{:S(2)}) collective-permute-start(f32[32,256]{1,0:T(8,128)S(1)} %convolution_add_fusion.15), channel_id=1, source_target_pairs={{64,0},{72,8},{80,16},{88,24},{96,32},{104,40},{112,48},{120,56},{... | collective-permute-start | bytes 98312 | tf_op jit(solution)/shard_map/ppermute | solution.py:12
  286.3 11.1 %collective-permute-start.20 = (f32[256,256]{1,0:T(8,128)S(1)}, f32[256,256]{1,0:T(8,128)S(1)}, u32[]{:S(2)}, u32[]{:S(2)}) collective-permute-start(f32[256,256]{1,0:T(8,128)S(1)} %fusion.61), channel_id=1, source_target_pairs={{64,0},{72,8},{80,16},{88,24},{96,32},{104,40},{112,48},{120,56},{... | collective-permute-start | bytes 786440 | tf_op jit(solution)/shard_map/ppermute | solution.py:12
  288.8 11.0 %collective-permute-start.19 = (f32[32,256]{1,0:T(8,128)S(1)}, f32[32,256]{1,0:T(8,128)S(1)}, u32[]{:S(2)}, u32[]{:S(2)}) collective-permute-start(f32[32,256]{1,0:T(8,128)S(1)} %convolution_add_fusion.14), channel_id=1, source_target_pairs={{128,0},{136,8},{144,16},{152,24},{160,32},{168,40},{176,48},{184,... | collective-permute-start | bytes 98312 | tf_op jit(solution)/shard_map/ppermute | solution.py:12
  297.8 17.0 %collective-permute-start.22 = (f32[256,256]{1,0:T(8,128)S(1)}, f32[256,256]{1,0:T(8,128)S(1)}, u32[]{:S(2)}, u32[]{:S(2)}) collective-permute-start(f32[256,256]{1,0:T(8,128)S(1)} %fusion.62), channel_id=1, source_target_pairs={{128,0},{136,8},{144,16},{152,24},{160,32},{168,40},{176,48},{184,... | collective-permute-start | bytes 786440 | tf_op jit(solution)/shard_map/ppermute | solution.py:12
  300.1 15.1 %collective-permute-start.21 = (f32[32,256]{1,0:T(8,128)S(1)}, f32[32,256]{1,0:T(8,128)S(1)}, u32[]{:S(2)}, u32[]{:S(2)}) collective-permute-start(f32[32,256]{1,0:T(8,128)S(1)} %convolution_add_fusion.13), channel_id=1, source_target_pairs={{256,0},{264,8},{272,16},{280,24},{288,32},{296,40},{304,48},{312,... | collective-permute-start | bytes 98312 | tf_op jit(solution)/shard_map/ppermute | solution.py:12
  514.4 9.6 %collective-permute-start.26 = (f32[32,256]{1,0:T(8,128)S(1)}, f32[32,256]{1,0:T(8,128)S(1)}, u32[]{:S(2)}, u32[]{:S(2)}) collective-permute-start(f32[32,256]{1,0:T(8,128)S(1)} %convolution_add_fusion.10), channel_id=1, source_target_pairs={{0,32},{8,40},{16,48},{24,56},{32,64},{40,72},{48,80},{56,88},{64,... | collective-permute-start | bytes 98312 | tf_op jit(solution)/shard_map/ppermute | solution.py:12
  539.9 9.7 %collective-permute-start.29 = (f32[32,256]{1,0:T(8,128)S(1)}, f32[32,256]{1,0:T(8,128)S(1)}, u32[]{:S(2)}, u32[]{:S(2)}) collective-permute-start(f32[32,256]{1,0:T(8,128)S(1)} %convolution_add_fusion.7), channel_id=1, source_target_pairs={{0,256},{8,264},{16,272},{24,280},{32,288},{40,296},{48,304},{56,3... | collective-permute-start | bytes 98312 | tf_op jit(solution)/shard_map/ppermute | solution.py:12
  635.6 17.8 %collective-permute-start.37 = (f32[32,256]{1,0:T(8,128)S(1)}, f32[32,256]{1,0:T(8,128)S(1)}, u32[]{:S(2)}, u32[]{:S(2)}) collective-permute-start(f32[32,256]{1,0:T(8,128)S(1)} %convolution_add_fusion), channel_id=1, source_target_pairs={{8,0},{16,8},{24,16},{32,24},{40,32},{48,40},{56,48},{64,56},{72,6... | collective-permute-start | bytes 98312 | tf_op jit(solution)/shard_map/ppermute | solution.py:12
  (18 other events, 257.0 us)
Sparse Core Ops, SparseCore 0:
  10.1 62.5 all-gather.1
where the time goes:
time: 818 us; the launch traced here: 812 us
  blocking collectives  258 us (32%)
  matrix products  221 us (27%)
  waiting for transfers between devices  214 us (26%)
  starting transfers between devices  95.2 us (12%)
  between operations  14.9 us (2%)
    dot_general x152, matrix products, transform(): lax.dot_general(vectors_in, matrix, (((1,), (1,)), ((), ())), precision=l...  175 us
    ppermute x38, waiting for transfers between devices, from_behind(): return lax.ppermute(block, axis, route)  148 us
    psum x1, blocking collectives, shards(): lax.psum(jnp.sum(second_solve * second_solve, axis=(0, 2)), 'chain')  129 us
    psum x1, blocking collectives, shards(): lax.psum(jnp.sum(first_solve * first_solve, axis=(0, 2)), 'chain')  129 us
    ppermute x38, starting transfers between devices, from_behind(): return lax.ppermute(block, axis, route)  95.2 us
    all_gather x1, waiting for transfers between devices, shards(): full_factors = lax.all_gather(factors, 'cols', axis=1, tiled=True)  64.7 us
    dot_general x42, matrix products, compose(): jnp.dot(later, earlier, precision=lax.Precision.HIGHEST, preferred_elemen...  46.4 us
  transfers between devices with their start and end apart: 39, of which 29 were waited for; matrix products, arithmetic and copies ran while one was open for 6% of the time, Pallas kernels for 0%

commit v1 on v0

--- a/solution.py
+++ b/solution.py
@@ -78,7 +78,14 @@
 
 
 def shards(start_vectors, factors):
-    full_factors = lax.all_gather(factors, "cols", axis=1, tiled=True)
+    slots = lax.axis_size("cols")
+    leaves = []
+    for ii in range(factors.ndim):
+        leaves.append(slots if ii == 1 else 1)
+    arr_next = jnp.tile(factors, leaves)
+    full_factors = lax.all_to_all(
+        arr_next, axis_name="cols", concat_axis=1, split_axis=1, tiled=True
+    )
 
     def pair_prefix(operator, summary, direction):
         sections = section_count()

time: 818 us -> 853 us (1.043)
  waiting for transfers between devices: 214 us -> 244 us
  between operations: 14.9 us -> 1.48 us
  local copies, waits for them, and re-layouts: 1.35 us -> 12.5 us
    all_to_all x0 -> x1, waiting for transfers between devices: none -> 96.2 us  [shards(): lax.all_to_all(arr_next, axis_name='cols', concat_axis=1, split_axis=1, t...]
    all_gather x1 -> x0, waiting for transfers between devices: 64.7 us -> none  [shards(): full_factors = lax.all_gather(factors, 'cols', axis=1, tiled=True)]
    all_to_all x0 -> x1, starting transfers between devices: none -> 10.3 us  [shards(): lax.all_to_all(arr_next, axis_name='cols', concat_axis=1, split_axis=1, t...]
    unnamed x7 -> x9, local copies, waits for them, and re-layouts: 0.03 us -> 8.66 us
where the time goes in v1:
time: 853 us; the launch traced here: 848 us
  blocking collectives  258 us (30%)
  waiting for transfers between devices  244 us (29%)
  matrix products  221 us (26%)
  starting transfers between devices  102 us (12%)
  local copies, waits for them, and re-layouts  12.5 us (1%)
    dot_general x152, matrix products, transform(): lax.dot_general(vectors_in, matrix, (((1,), (1,)), ((), ())), precision=l...  175 us
    ppermute x38, waiting for transfers between devices, from_behind(): return lax.ppermute(block, axis, route)  148 us
    psum x1, blocking collectives, shards(): lax.psum(jnp.sum(second_solve * second_solve, axis=(0, 2)), 'chain')  129 us
    psum x1, blocking collectives, shards(): lax.psum(jnp.sum(first_solve * first_solve, axis=(0, 2)), 'chain')  129 us
    all_to_all x1, waiting for transfers between devices, shards(): lax.all_to_all(arr_next, axis_name='cols', concat_axis=1, split_axis=1, t...  96.2 us
    ppermute x38, starting transfers between devices, from_behind(): return lax.ppermute(block, axis, route)  91.9 us
    dot_general x42, matrix products, compose(): jnp.dot(later, earlier, precision=lax.Precision.HIGHEST, preferred_elemen...  46.4 us
  transfers between devices with their start and end apart: 39, of which 29 were waited for; matrix products, arithmetic and copies ran while one was open for 6% of the time, Pallas kernels for 0%

profile of v1, /device:TPU:32, one launch (start us, length us, event | category | flops | bytes accessed | tf_op | source)
XLA Modules:
  0.0 847.9 jit_solution(10913627962332387379)
XLA Ops:
  4.5 10.3 %all-to-all-start = ((f32[16,256,256]{2,0,1:T(8,128)}), f32[16,256,256]{2,0,1:T(8,128)}, u32[]{:S(2)}, u32[]{:S(2)}) async-start(f32[16,256,256]{2,0,1:T(8,128)} %bitcast.211), calls=%async_computation | async-start | bytes 8388608 | tf_op jit(solution)/shard_map/all_to_all | solution.py:86
  14.8 96.2 %all-to-all-done = f32[16,256,256]{2,0,1:T(8,128)} async-done(((f32[16,256,256]{2,0,1:T(8,128)}), f32[16,256,256]{2,0,1:T(8,128)}, u32[]{:S(2)}, u32[]{:S(2)}) %all-to-all-start) | async-done | bytes 4194336 | tf_op jit(solution)/shard_map/all_to_all | solution.py:86
  117.6 21.4 %while.146 = (s32[]{:T(128)}, f32[32,256]{1,0:T(8,128)S(1)}, f32[16,256,256]{2,1,0:T(8,128)}, f32[16,32,256]{2,1,0:T(8,128)}, s32[]{:T(128)}, /*index=5*/s32[]{:T(128)}) while((s32[]{:T(128)}, f32[32,256]{1,0:T(8,128)S(1)}, f32[16,256,256]{2,1,0:T(8,128)}, f32[16,32,256]{2,1,0:T(8,128)}, s32[]{:T(128)}, /*index=5*/s32[]{:T(128)}) %tuple.251), condition=%wide.region_1.2_spmd.clone, body=%wide.region_0.1_spmd.clone.sunk | while | flops 25182212 | bytes 427087 | solution.py:38
  141.0 22.1 %while.138 = (s32[]{:T(128)}, f32[256,256]{1,0:T(8,128)S(1)}, f32[16,256,256]{2,1,0:T(8,128)}, s32[]{:T(128)}) while((s32[]{:T(128)}, f32[256,256]{1,0:T(8,128)S(1)}, f32[16,256,256]{2,1,0:T(8,128)}, s32[]{:T(128)}) %tuple.281), condition=%wide.region_3.4_spmd, body=%wide.region_2.3_spmd.sunk | while | flops 201326592 | bytes 1311285 | solution.py:57
  179.6 7.2 collective-permute-done.4
  191.4 10.8 %collective-permute-done.6 = f32[256,256]{1,0:T(8,128)S(1)} collective-permute-done((f32[256,256]{1,0:T(8,128)S(1)}, f32[256,256]{1,0:T(8,128)S(1)}, u32[]{:S(2)}, u32[]{:S(2)}) %collective-permute-start.6) | collective-permute-done | bytes 262176 | tf_op jit(solution)/shard_map/ppermute | solution.py:12
  206.8 7.4 collective-permute-done.8
  218.2 7.4 collective-permute-done.10
  235.6 21.4 %while.139 = (s32[]{:T(128)}, f32[32,256]{1,0:T(8,128)S(1)}, f32[16,32,256]{2,1,0:T(8,128)S(1)}, f32[16,256,256]{2,1,0:T(8,128)}, f32[16,32,256]{2,1,0:T(8,128)}, /*index=5*/s32[]{:T(128)}) while((s32[]{:T(128)}, f32[32,256]{1,0:T(8,128)S(1)}, f32[16,32,256]{2,1,0:T(8,128)S(1)}, f32[16,256,256]{2,1,0:T(8,128)}, f32[16,32,256]{2,1,0:T(8,128)}, ...), condition=%wide.region_5.6_spmd, body=%wide.region_4.5_spmd.sunk | while | flops 25174016 | bytes 459845 | solution.py:38
  257.0 21.3 %while.140 = (s32[]{:T(128)}, f32[32,256]{1,0:T(8,128)S(1)}, f32[16,32,256]{2,1,0:T(8,128)S(1)}, f32[16,256,256]{2,1,0:T(8,128)}, s32[]{:T(128)}, /*index=5*/s32[]{:T(128)}) while((s32[]{:T(128)}, f32[32,256]{1,0:T(8,128)S(1)}, f32[16,32,256]{2,1,0:T(8,128)S(1)}, f32[16,256,256]{2,1,0:T(8,128)}, s32[]{:T(128)}, /*index=5*/s32[]{:T(128)}) %tuple.283), condition=%wide.region_7.8_spmd, body=%wide.region_6.7_spmd.sunk | while | flops 25174020 | bytes 427089 | solution.py:48
  280.3 22.1 %while.141 = (s32[]{:T(128)}, f32[256,256]{1,0:T(8,128)S(1)}, f32[16,256,256]{2,1,0:T(8,128)}, s32[]{:T(128)}, s32[]{:T(128)}) while((s32[]{:T(128)}, f32[256,256]{1,0:T(8,128)S(1)}, f32[16,256,256]{2,1,0:T(8,128)}, s32[]{:T(128)}, s32[]{:T(128)}) %tuple.284), condition=%wide.region_9.10_spmd, body=%wide.region_8.9_spmd.sunk | while | flops 201326592 | bytes 1310797 | solution.py:57
  323.4 7.5 collective-permute-done.18
  346.6 13.5 %collective-permute-done.22 = f32[256,256]{1,0:T(8,128)S(1)} collective-permute-done((f32[256,256]{1,0:T(8,128)S(1)}, f32[256,256]{1,0:T(8,128)S(1)}, u32[]{:S(2)}, u32[]{:S(2)}) %collective-permute-start.22) | collective-permute-done | bytes 262176 | tf_op jit(solution)/shard_map/ppermute | solution.py:12
  365.0 21.6 %while.142 = (s32[]{:T(128)}, f32[32,256]{1,0:T(8,128)S(1)}, f32[16,32,256]{2,1,0:T(8,128)S(1)}, f32[16,32,256]{2,1,0:T(8,128)}, f32[16,256,256]{2,1,0:T(8,128)}, /*index=5*/s32[]{:T(128)}, s32[]{:T(128)}) while((s32[]{:T(128)}, f32[32,256]{1,0:T(8,128)S(1)}, f32[16,32,256]{2,1,0:T(8,128)S(1)}, f32[16,32,256]{2,1,0:T(8,128)}, ...), condition=%wide.region_11.12_spmd, body=%wide.region_10.11_spmd.sunk | while | flops 25174020 | bytes 460377 | solution.py:48
  386.8 129.1 %psum.14 = f32[32]{0:T(128)S(1)} all-reduce(f32[32]{0:T(128)S(1)} %multiply_reduce_fusion.1), channel_id=1, replica_groups=mesh['chain'=64,'cols'=8] {'chain'}, use_global_device_ids=true, to_apply=%region_13.14 | all-reduce | flops 32 | bytes 256 | tf_op jit(solution)/shard_map/psum | solution.py:111
  516.9 21.5 %while.147 = (s32[]{:T(128)}, f32[32,256]{1,0:T(8,128)S(1)}, f32[16,256,256]{2,1,0:T(8,128)}, f32[16,32,256]{2,1,0:T(8,128)}, s32[]{:T(128)}, /*index=5*/s32[]{:T(128)}) while((s32[]{:T(128)}, f32[32,256]{1,0:T(8,128)S(1)}, f32[16,256,256]{2,1,0:T(8,128)}, f32[16,32,256]{2,1,0:T(8,128)}, s32[]{:T(128)}, ...), condition=%wide.region_15.16_spmd.clone, body=%wide.region_14.15_spmd.clone.sunk | while | flops 25182212 | bytes 427087 | solution.py:38
  549.2 7.2 collective-permute-done.25
  558.8 7.5 collective-permute-done.26
  583.6 8.4 collective-permute-done.29
  600.9 21.4 %while.143 = (s32[]{:T(128)}, f32[32,256]{1,0:T(8,128)S(1)}, f32[16,32,256]{2,1,0:T(8,128)S(1)}, f32[16,256,256]{2,1,0:T(8,128)}, f32[16,32,256]{2,1,0:T(8,128)}, /*index=5*/s32[]{:T(128)}) while((s32[]{:T(128)}, f32[32,256]{1,0:T(8,128)S(1)}, f32[16,32,256]{2,1,0:T(8,128)S(1)}, f32[16,256,256]{2,1,0:T(8,128)}, f32[16,32,256]{2,1,0:T(8,128)}, ...), condition=%wide.region_17.18_spmd, body=%wide.region_16.17_spmd.sunk | while | flops 25174016 | bytes 459845 | solution.py:38
  622.4 21.3 %while.144 = (s32[]{:T(128)}, f32[32,256]{1,0:T(8,128)S(1)}, f32[16,32,256]{2,1,0:T(8,128)S(1)}, f32[16,256,256]{2,1,0:T(8,128)}, s32[]{:T(128)}, /*index=5*/s32[]{:T(128)}) while((s32[]{:T(128)}, f32[32,256]{1,0:T(8,128)S(1)}, f32[16,32,256]{2,1,0:T(8,128)S(1)}, f32[16,256,256]{2,1,0:T(8,128)}, s32[]{:T(128)}, /*index=5*/s32[]{:T(128)}) %tuple.288), condition=%wide.region_19.20_spmd, body=%wide.region_18.19_spmd.sunk | while | flops 25174020 | bytes 427089 | solution.py:48
  678.0 16.2 %collective-permute-start.37 = (f32[32,256]{1,0:T(8,128)S(1)}, f32[32,256]{1,0:T(8,128)S(1)}, u32[]{:S(2)}, u32[]{:S(2)}) collective-permute-start(f32[32,256]{1,0:T(8,128)S(1)} %convolution_add_fusion), channel_id=1, source_target_pairs={{8,0},{16,8},{24,16},{32,24},{40,32},{48,40},{56,48},{64,56},{72,6... | collective-permute-start | bytes 98312 | tf_op jit(solution)/shard_map/ppermute | solution.py:12
  695.9 21.3 %while.145 = (s32[]{:T(128)}, f32[32,256]{1,0:T(8,128)S(1)}, f32[16,32,256]{2,1,0:T(8,128)S(1)}, f32[16,32,256]{2,1,0:T(8,128)S(1)}, f32[16,256,256]{2,1,0:T(8,128)}, /*index=5*/s32[]{:T(128)}, s32[]{:T(128)}) while((s32[]{:T(128)}, f32[32,256]{1,0:T(8,128)S(1)}, f32[16,32,256]{2,1,0:T(8,128)S(1)}, f32[16,32,256]{2,1,0:T(8,128)S(1)}, ...), condition=%wide.region_21.22_spmd, body=%wide.region_20.21_spmd.sunk | while | flops 25174020 | bytes 460377 | solution.py:48
  717.3 129.1 %psum.15 = f32[32]{0:T(128)S(1)} all-reduce(f32[32]{0:T(128)S(1)} %multiply_reduce_fusion), channel_id=1, replica_groups=mesh['chain'=64,'cols'=8] {'chain'}, use_global_device_ids=true, to_apply=%region_23.24 | all-reduce | flops 32 | bytes 256 | tf_op jit(solution)/shard_map/psum | solution.py:116
  (445 shorter events, 383.6 us)
Async XLA Ops:
  4.5 106.6 %all-to-all-start = ((f32[16,256,256]{2,0,1:T(8,128)}), f32[16,256,256]{2,0,1:T(8,128)}, u32[]{:S(2)}, u32[]{:S(2)}) async-start(f32[16,256,256]{2,0,1:T(8,128)} %bitcast.211), calls=%async_computation | async-start | bytes 8388608 | tf_op jit(solution)/shard_map/all_to_all | solution.py:86
  139.0 27.5 %collective-permute-start = (f32[32,256]{1,0:T(8,128)S(1)}, f32[32,256]{1,0:T(8,128)S(1)}, u32[]{:S(2)}, u32[]{:S(2)}) collective-permute-start(f32[32,256]{1,0:T(8,128)S(1)} %get-tuple-element.568), channel_id=1, source_target_pairs={{0,8},{8,16},{16,24},{24,32},{32,40},{40,48},{48,56},{56,64},{64,7... | collective-permute-start | bytes 98312 | tf_op jit(solution)/shard_map/ppermute | solution.py:12
  163.1 11.0 %collective-permute-start.2 = (f32[256,256]{1,0:T(8,128)S(1)}, f32[256,256]{1,0:T(8,128)S(1)}, u32[]{:S(2)}, u32[]{:S(2)}) collective-permute-start(f32[256,256]{1,0:T(8,128)S(1)} %get-tuple-element.569), channel_id=1, source_target_pairs={{0,8},{8,16},{16,24},{24,32},{32,40},{40,48},{48,56},{56,64},{64,7... | collective-permute-start | bytes 786440 | tf_op jit(solution)/shard_map/ppermute | solution.py:12
  167.0 9.5 %collective-permute-start.1 = (f32[32,256]{1,0:T(8,128)S(1)}, f32[32,256]{1,0:T(8,128)S(1)}, u32[]{:S(2)}, u32[]{:S(2)}) collective-permute-start(f32[32,256]{1,0:T(8,128)S(1)} %convolution_add_fusion.23), channel_id=1, source_target_pairs={{0,16},{8,24},{16,32},{24,40},{32,48},{40,56},{48,64},{56,72},{64,... | collective-permute-start | bytes 98312 | tf_op jit(solution)/shard_map/ppermute | solution.py:12
  174.5 12.3 %collective-permute-start.4 = (f32[256,256]{1,0:T(8,128)S(1)}, f32[256,256]{1,0:T(8,128)S(1)}, u32[]{:S(2)}, u32[]{:S(2)}) collective-permute-start(f32[256,256]{1,0:T(8,128)S(1)} %fusion.54), channel_id=1, source_target_pairs={{0,16},{8,24},{16,32},{24,40},{32,48},{40,56},{48,64},{56,72},{64,... | collective-permute-start | bytes 786440 | tf_op jit(solution)/shard_map/ppermute | solution.py:12
  176.8 12.3 %collective-permute-start.3 = (f32[32,256]{1,0:T(8,128)S(1)}, f32[32,256]{1,0:T(8,128)S(1)}, u32[]{:S(2)}, u32[]{:S(2)}) collective-permute-start(f32[32,256]{1,0:T(8,128)S(1)} %convolution_add_fusion.22), channel_id=1, source_target_pairs={{0,32},{8,40},{16,48},{24,56},{32,64},{40,72},{48,80},{56,88},{64,... | collective-permute-start | bytes 98312 | tf_op jit(solution)/shard_map/ppermute | solution.py:12
  187.2 15.0 %collective-permute-start.6 = (f32[256,256]{1,0:T(8,128)S(1)}, f32[256,256]{1,0:T(8,128)S(1)}, u32[]{:S(2)}, u32[]{:S(2)}) collective-permute-start(f32[256,256]{1,0:T(8,128)S(1)} %fusion.55), channel_id=1, source_target_pairs={{0,32},{8,40},{16,48},{24,56},{32,64},{40,72},{48,80},{56,88},{64,... | collective-permute-start | bytes 786440 | tf_op jit(solution)/shard_map/ppermute | solution.py:12
  189.4 15.1 %collective-permute-start.5 = (f32[32,256]{1,0:T(8,128)S(1)}, f32[32,256]{1,0:T(8,128)S(1)}, u32[]{:S(2)}, u32[]{:S(2)}) collective-permute-start(f32[32,256]{1,0:T(8,128)S(1)} %convolution_add_fusion.21), channel_id=1, source_target_pairs={{0,64},{8,72},{16,80},{24,88},{32,96},{40,104},{48,112},{56,120},{... | collective-permute-start | bytes 98312 | tf_op jit(solution)/shard_map/ppermute | solution.py:12
  202.6 11.6 %collective-permute-start.8 = (f32[256,256]{1,0:T(8,128)S(1)}, f32[256,256]{1,0:T(8,128)S(1)}, u32[]{:S(2)}, u32[]{:S(2)}) collective-permute-start(f32[256,256]{1,0:T(8,128)S(1)} %fusion.56), channel_id=1, source_target_pairs={{0,64},{8,72},{16,80},{24,88},{32,96},{40,104},{48,112},{56,120},{... | collective-permute-start | bytes 786440 | tf_op jit(solution)/shard_map/ppermute | solution.py:12
  204.9 11.7 %collective-permute-start.7 = (f32[32,256]{1,0:T(8,128)S(1)}, f32[32,256]{1,0:T(8,128)S(1)}, u32[]{:S(2)}, u32[]{:S(2)}) collective-permute-start(f32[32,256]{1,0:T(8,128)S(1)} %convolution_add_fusion.20), channel_id=1, source_target_pairs={{0,128},{8,136},{16,144},{24,152},{32,160},{40,168},{48,176},{56,1... | collective-permute-start | bytes 98312 | tf_op jit(solution)/shard_map/ppermute | solution.py:12
  214.6 11.0 %collective-permute-start.10 = (f32[256,256]{1,0:T(8,128)S(1)}, f32[256,256]{1,0:T(8,128)S(1)}, u32[]{:S(2)}, u32[]{:S(2)}) collective-permute-start(f32[256,256]{1,0:T(8,128)S(1)} %fusion.57), channel_id=1, source_target_pairs={{0,128},{8,136},{16,144},{24,152},{32,160},{40,168},{48,176},{56,1... | collective-permute-start | bytes 786440 | tf_op jit(solution)/shard_map/ppermute | solution.py:12
  216.9 9.7 %collective-permute-start.9 = (f32[32,256]{1,0:T(8,128)S(1)}, f32[32,256]{1,0:T(8,128)S(1)}, u32[]{:S(2)}, u32[]{:S(2)}) collective-permute-start(f32[32,256]{1,0:T(8,128)S(1)} %convolution_add_fusion.19), channel_id=1, source_target_pairs={{0,256},{8,264},{16,272},{24,280},{32,288},{40,296},{48,304},{56,3... | collective-permute-start | bytes 98312 | tf_op jit(solution)/shard_map/ppermute | solution.py:12
  278.4 26.0 %collective-permute-start.12 = (f32[32,256]{1,0:T(8,128)S(1)}, f32[32,256]{1,0:T(8,128)S(1)}, u32[]{:S(2)}, u32[]{:S(2)}) collective-permute-start(f32[32,256]{1,0:T(8,128)S(1)} %get-tuple-element.571), channel_id=1, source_target_pairs={{8,0},{16,8},{24,16},{32,24},{40,32},{48,40},{56,48},{64,56},{72,6... | collective-permute-start | bytes 98312 | tf_op jit(solution)/shard_map/ppermute | solution.py:12
  309.0 9.8 %collective-permute-start.16 = (f32[256,256]{1,0:T(8,128)S(1)}, f32[256,256]{1,0:T(8,128)S(1)}, u32[]{:S(2)}, u32[]{:S(2)}) collective-permute-start(f32[256,256]{1,0:T(8,128)S(1)} %fusion.59), channel_id=1, source_target_pairs={{16,0},{24,8},{32,16},{40,24},{48,32},{56,40},{64,48},{72,56},{80,... | collective-permute-start | bytes 786440 | tf_op jit(solution)/shard_map/ppermute | solution.py:12
  311.8 9.2 %collective-permute-start.15 = (f32[32,256]{1,0:T(8,128)S(1)}, f32[32,256]{1,0:T(8,128)S(1)}, u32[]{:S(2)}, u32[]{:S(2)}) collective-permute-start(f32[32,256]{1,0:T(8,128)S(1)} %convolution_add_fusion.16), channel_id=1, source_target_pairs={{32,0},{40,8},{48,16},{56,24},{64,32},{72,40},{80,48},{88,56},{96,... | collective-permute-start | bytes 98312 | tf_op jit(solution)/shard_map/ppermute | solution.py:12
  319.2 11.7 %collective-permute-start.18 = (f32[256,256]{1,0:T(8,128)S(1)}, f32[256,256]{1,0:T(8,128)S(1)}, u32[]{:S(2)}, u32[]{:S(2)}) collective-permute-start(f32[256,256]{1,0:T(8,128)S(1)} %fusion.60), channel_id=1, source_target_pairs={{32,0},{40,8},{48,16},{56,24},{64,32},{72,40},{80,48},{88,56},{96,... | collective-permute-start | bytes 786440 | tf_op jit(solution)/shard_map/ppermute | solution.py:12
  321.4 12.0 %collective-permute-start.17 = (f32[32,256]{1,0:T(8,128)S(1)}, f32[32,256]{1,0:T(8,128)S(1)}, u32[]{:S(2)}, u32[]{:S(2)}) collective-permute-start(f32[32,256]{1,0:T(8,128)S(1)} %convolution_add_fusion.15), channel_id=1, source_target_pairs={{64,0},{72,8},{80,16},{88,24},{96,32},{104,40},{112,48},{120,56},{... | collective-permute-start | bytes 98312 | tf_op jit(solution)/shard_map/ppermute | solution.py:12
  331.2 11.2 %collective-permute-start.20 = (f32[256,256]{1,0:T(8,128)S(1)}, f32[256,256]{1,0:T(8,128)S(1)}, u32[]{:S(2)}, u32[]{:S(2)}) collective-permute-start(f32[256,256]{1,0:T(8,128)S(1)} %fusion.61), channel_id=1, source_target_pairs={{64,0},{72,8},{80,16},{88,24},{96,32},{104,40},{112,48},{120,56},{... | collective-permute-start | bytes 786440 | tf_op jit(solution)/shard_map/ppermute | solution.py:12
  333.8 11.1 %collective-permute-start.19 = (f32[32,256]{1,0:T(8,128)S(1)}, f32[32,256]{1,0:T(8,128)S(1)}, u32[]{:S(2)}, u32[]{:S(2)}) collective-permute-start(f32[32,256]{1,0:T(8,128)S(1)} %convolution_add_fusion.14), channel_id=1, source_target_pairs={{128,0},{136,8},{144,16},{152,24},{160,32},{168,40},{176,48},{184,... | collective-permute-start | bytes 98312 | tf_op jit(solution)/shard_map/ppermute | solution.py:12
  342.8 17.2 %collective-permute-start.22 = (f32[256,256]{1,0:T(8,128)S(1)}, f32[256,256]{1,0:T(8,128)S(1)}, u32[]{:S(2)}, u32[]{:S(2)}) collective-permute-start(f32[256,256]{1,0:T(8,128)S(1)} %fusion.62), channel_id=1, source_target_pairs={{128,0},{136,8},{144,16},{152,24},{160,32},{168,40},{176,48},{184,... | collective-permute-start | bytes 786440 | tf_op jit(solution)/shard_map/ppermute | solution.py:12
  345.3 15.2 %collective-permute-start.21 = (f32[32,256]{1,0:T(8,128)S(1)}, f32[32,256]{1,0:T(8,128)S(1)}, u32[]{:S(2)}, u32[]{:S(2)}) collective-permute-start(f32[32,256]{1,0:T(8,128)S(1)} %convolution_add_fusion.13), channel_id=1, source_target_pairs={{256,0},{264,8},{272,16},{280,24},{288,32},{296,40},{304,48},{312,... | collective-permute-start | bytes 98312 | tf_op jit(solution)/shard_map/ppermute | solution.py:12
  556.7 9.6 %collective-permute-start.26 = (f32[32,256]{1,0:T(8,128)S(1)}, f32[32,256]{1,0:T(8,128)S(1)}, u32[]{:S(2)}, u32[]{:S(2)}) collective-permute-start(f32[32,256]{1,0:T(8,128)S(1)} %convolution_add_fusion.10), channel_id=1, source_target_pairs={{0,32},{8,40},{16,48},{24,56},{32,64},{40,72},{48,80},{56,88},{64,... | collective-permute-start | bytes 98312 | tf_op jit(solution)/shard_map/ppermute | solution.py:12
  582.3 9.7 %collective-permute-start.29 = (f32[32,256]{1,0:T(8,128)S(1)}, f32[32,256]{1,0:T(8,128)S(1)}, u32[]{:S(2)}, u32[]{:S(2)}) collective-permute-start(f32[32,256]{1,0:T(8,128)S(1)} %convolution_add_fusion.7), channel_id=1, source_target_pairs={{0,256},{8,264},{16,272},{24,280},{32,288},{40,296},{48,304},{56,3... | collective-permute-start | bytes 98312 | tf_op jit(solution)/shard_map/ppermute | solution.py:12
  678.0 17.8 %collective-permute-start.37 = (f32[32,256]{1,0:T(8,128)S(1)}, f32[32,256]{1,0:T(8,128)S(1)}, u32[]{:S(2)}, u32[]{:S(2)}) collective-permute-start(f32[32,256]{1,0:T(8,128)S(1)} %convolution_add_fusion), channel_id=1, source_target_pairs={{8,0},{16,8},{24,16},{32,24},{40,32},{48,40},{56,48},{64,56},{72,6... | collective-permute-start | bytes 98312 | tf_op jit(solution)/shard_map/ppermute | solution.py:12
  (18 other events, 248.3 us)
